TPU v7x, 32 devices: a whole 2x2x4 slice. The times are simulated.
32 devices in a mesh: dp: 16 (over z, y, x), tensor: 2 (over core).
Axes of the slice: x: 2, y: 2, z: 4, core: 2. Of those that a mesh axis runs over, the one named last changes fastest.
Arguments:
- tokens: bfloat16 [16384, 768], P('dp'), may hold values from -6 to 6
- cotangent: bfloat16 [16384, 768], P('dp'), may hold values from -6 to 6
- lengths: int32 [32], P('dp'), may hold values from 113 to 512, as said below
- proj_weight: float32 [2, 768, 3, 768], P(None, 'dp', None, 'tensor'), may hold values from -0.21875 to 0.21875
- out_weight: float32 [2, 768, 768], P(None, 'dp', 'tensor'), may hold values from -0.875 to 0.875
- up_weight: float32 [2, 768, 3072], P(None, 'dp', 'tensor'), may hold values from -0.21875 to 0.21875
- down_weight: float32 [2, 768, 3072], P(None, 'dp', 'tensor'), may hold values from -0.109375 to 0.109375
- small_params: float32 [2, 8448], replicated, may hold values from -0.8 to 1.4
- proj_first: float32 [2, 768, 3, 768], P(None, 'dp', None, 'tensor'), may hold values from -0.00018310547 to 0.00018310547
- proj_second: float32 [2, 768, 3, 768], P(None, 'dp', None, 'tensor'), may hold values from 3.527916e-11 to 3.52791626e-09
- out_first: float32 [2, 768, 768], P(None, 'dp', 'tensor'), may hold values from -0.00018310547 to 0.00018310547
- out_second: float32 [2, 768, 768], P(None, 'dp', 'tensor'), may hold values from 7.0558325e-12 to 7.0558325e-10
- up_first: float32 [2, 768, 3072], P(None, 'dp', 'tensor'), may hold values from -0.00018310547 to 0.00018310547
- up_second: float32 [2, 768, 3072], P(None, 'dp', 'tensor'), may hold values from 3.527916e-11 to 3.52791626e-09
- down_first: float32 [2, 768, 3072], P(None, 'dp', 'tensor'), may hold values from -0.00018310547 to 0.00018310547
- down_second: float32 [2, 768, 3072], P(None, 'dp', 'tensor'), may hold values from 3.527916e-11 to 3.52791626e-09
- small_first: float32 [2, 8448], replicated, may hold values from -0.00018310547 to 0.00018310547
- small_second: float32 [2, 8448], replicated, may hold values from 3.527916e-11 to 5.644666e-10
Outputs:
- activations: float32 [16384, 768], P('dp')
- input_grad: float32 [16384, 768], P('dp')
- grad_norm: float32 [], replicated
- proj_first_new: float32 [2, 768, 3, 768], P(None, 'dp', None, 'tensor')
- proj_second_new: float32 [2, 768, 3, 768], P(None, 'dp', None, 'tensor')
- proj_weight_new: float32 [2, 768, 3, 768], P(None, 'dp', None, 'tensor')
- out_first_new: float32 [2, 768, 768], P(None, 'dp', 'tensor')
- out_second_new: float32 [2, 768, 768], P(None, 'dp', 'tensor')
- out_weight_new: float32 [2, 768, 768], P(None, 'dp', 'tensor')
- up_first_new: float32 [2, 768, 3072], P(None, 'dp', 'tensor')
- up_second_new: float32 [2, 768, 3072], P(None, 'dp', 'tensor')
- up_weight_new: float32 [2, 768, 3072], P(None, 'dp', 'tensor')
- down_first_new: float32 [2, 768, 3072], P(None, 'dp', 'tensor')
- down_second_new: float32 [2, 768, 3072], P(None, 'dp', 'tensor')
- down_weight_new: float32 [2, 768, 3072], P(None, 'dp', 'tensor')
- small_first_new: float32 [2, 8448], replicated
- small_second_new: float32 [2, 8448], replicated
- small_params_new: float32 [2, 8448], replicated
Inputs may be any that keep to these rules, and one draw needn't show every extreme that they name: `lengths`: each length is 512, 256 or 128, reduced by less than max(1, 16); the first sequence has length 512.
All inputs are finite; a program needn't handle non-finite values.
Results may differ from a plain program's by a relative error of at most 0.03.
The roundings to bfloat16 on the way count: a program that leaves them out, or rounds other values in their place, can miss the bound.
Values may be sent and summed in bfloat16 or wider, within the bound.
No kernel may reach another device: no remote copies, remote signals or barrier semaphores. Data moves between devices by JAX's collectives and lax.ppermute only.
A program may use at most 192 MiB of HBM per device.

v0:
```python
from functools import partial
import math
import jax
import jax.numpy as jnp
from jax import lax
from jax.sharding import PartitionSpec as P

D = 768
HEADS = 12
FF = 3072
beta_one = 0.9
beta_two = 0.999
adam_eps = 1e-06
decay_rate = 0.01
matrix_rate = 1.0
vector_rate = 0.3
clip_norm = 1.0
step_count = 10.0
norm_eps = 1e-06
masked_score = -1e30


def layer_norm(values, norm_gain, norm_shift):
    average = jnp.mean(values, axis=-1, keepdims=True)
    centered = values - average
    variance = jnp.mean(centered * centered, axis=-1, keepdims=True)
    return centered * lax.rsqrt(variance + norm_eps) * norm_gain + norm_shift


def split_vector(packed):
    bounds = [0, D, 2 * D, 2 * D + FF, 3 * D + FF, 4 * D + FF, 5 * D + FF, 6 * D + FF, 7 * D + FF]
    return [packed[bounds[place] : bounds[place + 1]] for place in range(8)]


def head_scores(query, keys, score_scale):
    return jnp.einsum("qhe,khe->hqk", query, keys, preferred_element_type=jnp.float32) * score_scale


def total_scores(pairs, score_scale):
    score_total = head_scores(pairs[0], pairs[1], score_scale)
    for place in range(2, len(pairs), 2):
        score_total = score_total + head_scores(pairs[place], pairs[place + 1], score_scale)
    return score_total


def attend_forward(block_item, score_scale):
    key_valid, value_rows = (block_item[0], block_item[1])
    score_total = total_scores(block_item[2:], score_scale)
    masked = jnp.where(key_valid[None, None, :], score_total, masked_score)
    row_max = jnp.max(masked, axis=-1, keepdims=True)
    exp_terms = jnp.exp(masked - row_max)
    row_sum = jnp.sum(exp_terms, axis=-1, keepdims=True)
    soft_low = (exp_terms / row_sum).astype(jnp.bfloat16)
    context = jnp.einsum("hqk,khe->qhe", soft_low, value_rows, preferred_element_type=jnp.float32)
    return (context.astype(jnp.bfloat16), (row_max + jnp.log(row_sum))[..., 0])


def attend_backward(block_item, score_scale, with_later, keep_total):
    key_valid, value_rows, log_norm, context_grad = (
        block_item[0],
        block_item[1],
        block_item[2],
        block_item[3],
    )
    rest = block_item[4:]
    if with_later:
        later = rest[0]
        pairs = rest[1:]
    else:
        pairs = rest
    score_total = total_scores(pairs, score_scale)
    soft = jnp.where(key_valid[None, None, :], jnp.exp(score_total - log_norm[..., None]), 0.0)
    soft_grad = jnp.einsum(
        "qhe,khe->hqk", context_grad, value_rows, preferred_element_type=jnp.float32
    )
    total_grad = soft * (soft_grad - jnp.sum(soft * soft_grad, axis=-1, keepdims=True))
    if with_later:
        total_grad = total_grad + later
    total_low = total_grad.astype(jnp.bfloat16)
    query_grad = (
        jnp.einsum("hqk,khe->qhe", total_low, pairs[1], preferred_element_type=jnp.float32)
        * score_scale
    )
    key_grad = (
        jnp.einsum("hqk,qhe->khe", total_low, pairs[0], preferred_element_type=jnp.float32)
        * score_scale
    )
    value_grad = jnp.einsum(
        "hqk,qhe->khe", soft.astype(jnp.bfloat16), context_grad, preferred_element_type=jnp.float32
    )
    results = (query_grad, key_grad, value_grad)
    if keep_total:
        results = results + (total_grad,)
    return results


def adam_parts(gradient, first, second, factor):
    clipped = gradient * factor
    first_new = beta_one * first + (1.0 - beta_one) * clipped
    second_new = beta_two * second + (1.0 - beta_two) * clipped * clipped
    first_hat = first_new / (1.0 - beta_one**step_count)
    second_hat = second_new / (1.0 - beta_two**step_count)
    return (first_new, second_new, first_hat / (jnp.sqrt(second_hat) + adam_eps))


def local(
    tokens,
    cotangent,
    lengths,
    proj_weight,
    out_weight,
    up_weight,
    down_weight,
    small_params,
    proj_first,
    proj_second,
    out_first,
    out_second,
    up_first,
    up_second,
    down_first,
    down_second,
    small_first,
    small_second,
):
    layers = proj_weight.shape[0]
    seq_count = lengths.shape[0]
    seq_len = tokens.shape[0] // seq_count
    local_width = proj_weight.shape[3]
    head_dim = D // HEADS
    local_heads = local_width // head_dim
    hidden_local = up_weight.shape[2]
    score_scale = 1.0 / math.sqrt(head_dim)
    share_scale = 1.0 / lax.axis_size("tensor")
    tensor_rank = lax.axis_index("tensor")
    proj_full, out_full, up_full, down_full = (
        lax.all_gather(proj_weight.astype(jnp.bfloat16), "dp", axis=1, tiled=True),
        lax.all_gather(out_weight.astype(jnp.bfloat16), "dp", axis=1, tiled=True),
        lax.all_gather(up_weight.astype(jnp.bfloat16), "dp", axis=1, tiled=True),
        lax.all_gather(down_weight.astype(jnp.bfloat16), "dp", axis=1, tiled=True),
    )
    positions = jnp.arange(seq_len)
    key_valid = positions[None, :] < lengths[:, None]
    row_valid = key_valid.reshape(-1, 1)

    def own_part(vector, width):
        return lax.dynamic_slice_in_dim(vector, tensor_rank * width, width)

    def place_part(local_values, full_width):
        return lax.dynamic_update_slice_in_dim(
            jnp.zeros((full_width,), jnp.float32),
            local_values,
            tensor_rank * local_values.shape[0],
            0,
        )

    def heads_view(rows):
        return rows.reshape(seq_count, seq_len, local_heads, head_dim)

    hidden = tokens.astype(jnp.float32)
    saved = []
    for layer_at in range(layers):
        bias_v, bias_o, bias_up, bias_down, gain_one, shift_one, gain_two, shift_two = split_vector(
            small_params[layer_at]
        )
        input_low = hidden.astype(jnp.bfloat16)
        projected = jnp.einsum(
            "td,dcf->tcf", input_low, proj_full[layer_at], preferred_element_type=jnp.float32
        )
        query_low = projected[:, 0].astype(jnp.bfloat16)
        key_low = projected[:, 1].astype(jnp.bfloat16)
        value_low = (projected[:, 2] + own_part(bias_v, local_width)).astype(jnp.bfloat16)
        pairs = [heads_view(query_low), heads_view(key_low)]
        for earlier in reversed(saved):
            pairs += [heads_view(earlier["query"]), heads_view(earlier["keys"])]
        context_low, log_norm = lax.map(
            partial(attend_forward, score_scale=score_scale),
            (key_valid, heads_view(value_low)) + tuple(pairs),
        )
        context_low = context_low.reshape(-1, local_width)
        attended = lax.psum(
            jnp.einsum(
                "tf,df->td", context_low, out_full[layer_at], preferred_element_type=jnp.float32
            ).astype(jnp.bfloat16),
            "tensor",
        ).astype(jnp.float32)
        first_in = hidden + attended + bias_o
        first_out = layer_norm(first_in, gain_one, shift_one)
        first_low = first_out.astype(jnp.bfloat16)
        before_act = jnp.einsum(
            "td,df->tf", first_low, up_full[layer_at], preferred_element_type=jnp.float32
        ) + own_part(bias_up, hidden_local)
        act_low = jax.nn.gelu(before_act, approximate=False).astype(jnp.bfloat16)
        returned = lax.psum(
            jnp.einsum(
                "tf,df->td", act_low, down_full[layer_at], preferred_element_type=jnp.float32
            ).astype(jnp.bfloat16),
            "tensor",
        ).astype(jnp.float32)
        second_in = first_out + returned + bias_down
        saved.append(
            {
                "layer_input": input_low,
                "query": query_low,
                "keys": key_low,
                "value_rows": value_low,
                "log_norm": log_norm,
                "context": context_low,
                "first_in": first_in,
                "first_low": first_low,
                "before_act": before_act,
                "act_low": act_low,
                "second_in": second_in,
            }
        )
        hidden = layer_norm(second_in, gain_two, shift_two)
    grad_rows = jnp.where(row_valid, cotangent.astype(jnp.float32), 0.0)
    proj_grads = [None] * layers
    out_grads = [None] * layers
    up_grads = [None] * layers
    down_grads = [None] * layers
    small_grads = [None] * layers
    later_total = None
    for layer_at in reversed(range(layers)):
        kept = saved[layer_at]
        bias_v, bias_o, bias_up, bias_down, gain_one, shift_one, gain_two, shift_two = split_vector(
            small_params[layer_at]
        )
        second_in_grad, gain_two_grad, shift_two_grad = jax.vjp(
            layer_norm, kept["second_in"], gain_two, shift_two
        )[1](grad_rows)
        down_in_low = second_in_grad.astype(jnp.bfloat16)
        down_grads[layer_at] = jnp.einsum(
            "td,tf->df", down_in_low, kept["act_low"], preferred_element_type=jnp.float32
        )
        act_grad = jnp.einsum(
            "td,df->tf", down_in_low, down_full[layer_at], preferred_element_type=jnp.float32
        )
        before_grad = jax.vjp(partial(jax.nn.gelu, approximate=False), kept["before_act"])[1](
            act_grad
        )[0]
        before_low = before_grad.astype(jnp.bfloat16)
        up_grads[layer_at] = jnp.einsum(
            "td,tf->df", kept["first_low"], before_low, preferred_element_type=jnp.float32
        )
        first_back = lax.psum(
            jnp.einsum(
                "tf,df->td", before_low, up_full[layer_at], preferred_element_type=jnp.float32
            ).astype(jnp.bfloat16),
            "tensor",
        ).astype(jnp.float32)
        first_out_grad = second_in_grad + first_back
        first_in_grad, gain_one_grad, shift_one_grad = jax.vjp(
            layer_norm, kept["first_in"], gain_one, shift_one
        )[1](first_out_grad)
        out_in_low = first_in_grad.astype(jnp.bfloat16)
        out_grads[layer_at] = jnp.einsum(
            "td,tf->df", out_in_low, kept["context"], preferred_element_type=jnp.float32
        )
        context_grad = jnp.einsum(
            "td,df->tf", out_in_low, out_full[layer_at], preferred_element_type=jnp.float32
        ).astype(jnp.bfloat16)
        pairs = [heads_view(kept["query"]), heads_view(kept["keys"])]
        for earlier in reversed(saved[:layer_at]):
            pairs += [heads_view(earlier["query"]), heads_view(earlier["keys"])]
        items = (
            key_valid,
            heads_view(kept["value_rows"]),
            kept["log_norm"],
            heads_view(context_grad),
        )
        with_later = later_total is not None
        if with_later:
            items = items + (later_total,)
        items = items + tuple(pairs)
        results = lax.map(
            partial(
                attend_backward,
                score_scale=score_scale,
                with_later=with_later,
                keep_total=layer_at > 0,
            ),
            items,
        )
        later_total = results[3] if layer_at > 0 else None
        query_grad = results[0].reshape(-1, local_width)
        key_grad = results[1].reshape(-1, local_width)
        value_grad = results[2].reshape(-1, local_width)
        proj_grad_low = jnp.stack([query_grad, key_grad, value_grad], axis=1).astype(jnp.bfloat16)
        proj_grads[layer_at] = jnp.einsum(
            "td,tcf->dcf", kept["layer_input"], proj_grad_low, preferred_element_type=jnp.float32
        )
        input_back = lax.psum(
            jnp.einsum(
                "tcf,dcf->td",
                proj_grad_low,
                proj_full[layer_at],
                preferred_element_type=jnp.float32,
            ).astype(jnp.bfloat16),
            "tensor",
        ).astype(jnp.float32)
        grad_rows = first_in_grad + input_back
        small_grads[layer_at] = jnp.concatenate(
            [
                place_part(jnp.sum(value_grad, axis=0), D),
                share_scale * jnp.sum(first_in_grad, axis=0),
                place_part(jnp.sum(before_grad, axis=0), FF),
                share_scale * jnp.sum(second_in_grad, axis=0),
                share_scale * gain_one_grad,
                share_scale * shift_one_grad,
                share_scale * gain_two_grad,
                share_scale * shift_two_grad,
            ]
        )
    big_totals = (
        jnp.stack(proj_grads),
        jnp.stack(out_grads),
        jnp.stack(up_grads),
        jnp.stack(down_grads),
    )
    small_partial = jnp.stack(small_grads)
    row_count = proj_weight.shape[1]
    summed = lax.psum((big_totals[0], big_totals[1], big_totals[2], big_totals[3]), "dp")
    row_start = lax.axis_index("dp") * row_count
    shares = tuple(
        (lax.dynamic_slice_in_dim(summed_part, row_start, row_count, 1) for summed_part in summed)
    )
    masters = (proj_weight, out_weight, up_weight, down_weight)
    firsts = (proj_first, out_first, up_first, down_first)
    seconds = (proj_second, out_second, up_second, down_second)
    square_part = jnp.sum(shares[0] * shares[0])
    for kind_at in range(1, 4):
        square_part = square_part + jnp.sum(shares[kind_at] * shares[kind_at])
    weight_square = jnp.stack(
        [jnp.sum(master * master, axis=tuple(range(1, master.ndim))) for master in masters]
    )
    square_big, weight_square, small_grad = lax.psum(
        (square_part, weight_square, small_partial), ("dp", "tensor")
    )
    grad_norm = jnp.sqrt(square_big + jnp.sum(small_grad * small_grad))
    factor = clip_norm / jnp.maximum(grad_norm, clip_norm)
    moments = []
    updates = []
    for kind_at in range(4):
        first_new, second_new, direction = adam_parts(
            shares[kind_at], firsts[kind_at], seconds[kind_at], factor
        )
        moments.append((first_new, second_new))
        updates.append(direction + decay_rate * masters[kind_at])
    update_square = jnp.stack(
        [jnp.sum(update * update, axis=tuple(range(1, update.ndim))) for update in updates]
    )
    update_square = lax.psum(update_square, ("dp", "tensor"))
    ratio = jnp.sqrt(weight_square) / jnp.sqrt(update_square)
    outputs = [hidden, grad_rows, grad_norm]
    for kind_at in range(4):
        master = masters[kind_at]
        scaled = ratio[kind_at].reshape((-1,) + (1,) * (master.ndim - 1))
        outputs += [
            moments[kind_at][0],
            moments[kind_at][1],
            master - matrix_rate * scaled * updates[kind_at],
        ]
    small_first_new, small_second_new, small_direction = adam_parts(
        small_grad, small_first, small_second, factor
    )
    outputs += [small_first_new, small_second_new, small_params - vector_rate * small_direction]
    return tuple(outputs)


def solution(mesh):
    placed = (
        P("dp", None),
        P("dp", None),
        P("dp"),
        P(None, "dp", None, "tensor"),
        P(None, "dp", "tensor"),
        P(None, "dp", "tensor"),
        P(None, "dp", "tensor"),
        P(),
        P(None, "dp", None, "tensor"),
        P(None, "dp", None, "tensor"),
        P(None, "dp", "tensor"),
        P(None, "dp", "tensor"),
        P(None, "dp", "tensor"),
        P(None, "dp", "tensor"),
        P(None, "dp", "tensor"),
        P(None, "dp", "tensor"),
        P(),
        P(),
    )
    return jax.shard_map(
        local,
        mesh=mesh,
        in_specs=placed,
        out_specs=(
            P("dp", None),
            P("dp", None),
            P(),
            P(None, "dp", None, "tensor"),
            P(None, "dp", None, "tensor"),
            P(None, "dp", None, "tensor"),
            P(None, "dp", "tensor"),
            P(None, "dp", "tensor"),
            P(None, "dp", "tensor"),
            P(None, "dp", "tensor"),
            P(None, "dp", "tensor"),
            P(None, "dp", "tensor"),
            P(None, "dp", "tensor"),
            P(None, "dp", "tensor"),
            P(None, "dp", "tensor"),
            P(),
            P(),
            P(),
        ),
        check_vma=False,
    )
```

profile of v0, /device:TPU:0, one launch (start us, length us, event | category | flops | bytes accessed | tf_op | source)
XLA Modules:
  0.0 1741.2 jit_solution(10675762374318251473)
XLA Ops:
  13.1 72.2 %all-gather.5.cloned.1.call-done = bf16[2,768,3,384]{3,1,2,0:T(8,128)(2,1)} async-done(((bf16[2,48,3,384]{3,1,2,0:T(8,128)(2,1)}), bf16[2,768,3,384]{3,1,2,0:T(8,128)(2,1)}) %all-gather.5.cloned.1.call-update) | async-done | bytes 3538960 | tf_op jit(solution)/shard_map/all_gather | solution.py:137
  85.3 5.6 fusion.209
  103.5 11.4 while.54
  116.8 26.5 %all-gather.7.cloned.1.call-done = bf16[2,768,384]{2,1,0:T(8,128)(2,1)} async-done(((bf16[2,48,384]{2,1,0:T(8,128)(2,1)}), bf16[2,768,384]{2,1,0:T(8,128)(2,1)}) %all-gather.7.cloned.1.call-update) | async-done | bytes 1179664 | tf_op jit(solution)/shard_map/all_gather | solution.py:138
  143.3 3.6 convolution_convert_fusion.1
  150.6 15.8 all-reduce.13.cloned.1.call-done
  169.4 82.1 %all-gather.9.cloned.1.call-done = bf16[2,768,1536]{2,1,0:T(8,128)(2,1)} async-done(((bf16[2,48,1536]{2,1,0:T(8,128)(2,1)}), bf16[2,768,1536]{2,1,0:T(8,128)(2,1)}) %all-gather.9.cloned.1.call-update) | async-done | bytes 4718608 | tf_op jit(solution)/shard_map/all_gather | solution.py:139
  251.5 20.8 %multiply_convert_fusion.1 = (bf16[1024,1536]{1,0:T(8,128)(2,1)}, f32[1024,1536]{1,0:T(8,128)}, f32[1024,1536]{1,0:T(8,128)}) fusion(f32[1536]{0:T(1024)S(1)} %dynamic-slice_reduce_fusion.5, bf16[2,768,1536]{2,1,0:T(8,128)(2,1)} %all-gather.9.cloned.1.call-done, f32[768]{0:T(1024)S(1)} %get-tuple-element.431, f32[768]{0:T(1024)S(1)} %get-tuple-element.432, ...), kind=kOutput, calls=%fused_computation.155 | convolution fusion | flops 2526806016 | bytes 21257216 | tf_op jit(solution)/shard_map/td,df->tf/dot_general | solution.py:190
  272.3 61.6 %all-gather.11.cloned.1.call-done = bf16[2,768,1536]{2,1,0:T(8,128)(2,1)} async-done(((bf16[2,48,1536]{2,1,0:T(8,128)(2,1)}), bf16[2,768,1536]{2,1,0:T(8,128)(2,1)}) %all-gather.11.cloned.1.call-update) | async-done | bytes 4718608 | tf_op jit(solution)/shard_map/all_gather | solution.py:140
  333.9 6.4 fusion.151
  340.5 19.1 %all-reduce.15.cloned.1.call-done = bf16[1024,768]{1,0:T(8,128)(2,1)} async-done(((bf16[1024,768]{1,0:T(8,128)(2,1)}), bf16[1024,768]{1,0:T(8,128)(2,1)}) %all-reduce.15.cloned.1.call-update) | async-done | bytes 1572880 | tf_op jit(solution)/shard_map/psum | solution.py:194
  359.6 3.6 fusion.200
  363.7 3.8 fusion.210
  380.8 14.3 while.55
  382.3 2.8 fusion.280
  389.2 2.8 fusion.280
  400.4 21.7 %all-reduce.17.cloned.1.call-done = bf16[1024,768]{1,0:T(8,128)(2,1)} async-done(((bf16[1024,768]{1,0:T(8,128)(2,1)}), bf16[1024,768]{1,0:T(8,128)(2,1)}) %all-reduce.17.cloned.1.call-update) | async-done | bytes 1572880 | tf_op jit(solution)/shard_map/psum | solution.py:181
  422.1 3.6 fusion.199
  426.5 18.6 %multiply_convert_fusion = (bf16[1024,1536]{1,0:T(8,128)(2,1)S(1)}, f32[1024,1536]{1,0:T(8,128)}, f32[1024,1536]{1,0:T(8,128)}) fusion(f32[1536]{0:T(1024)S(1)} %dynamic-slice_reduce_fusion.4, bf16[2,768,1536]{2,1,0:T(8,128)(2,1)S(1)} %bitcast.417, f32[1024,768]{1,0:T(8,128)S(1)} %get-tuple-element.545, f32[768]{0:T(1024)S(1)} %copy-done.104, ...), kind=kOutput, calls=%fused_computation.142 | convolution fusion | flops 2523660288 | bytes 21258240 | tf_op jit(solution)/shard_map/td,df->tf/dot_general | solution.py:190
  446.8 5.4 fusion.149
  452.2 21.7 %all-reduce.19.cloned.1.call-done = bf16[1024,768]{1,0:T(8,128)(2,1)} async-done(((bf16[1024,768]{1,0:T(8,128)(2,1)}), bf16[1024,768]{1,0:T(8,128)(2,1)}) %all-reduce.19.cloned.1.call-update) | async-done | bytes 1572880 | tf_op jit(solution)/shard_map/psum | solution.py:194
  473.9 3.6 fusion.197
  481.4 2.9 fusion.196
  484.4 9.5 fusion.211
  495.6 3.7 fusion.150
  503.6 8.0 convolution_bitcast_fusion.2
  511.6 9.5 all-reduce.21.cloned.1.call-done
  521.1 4.9 multiply_reduce_fusion.3
  534.4 3.3 reshape.326
  541.2 36.4 %while.56 = (s32[]{:T(128)}, bf16[2,512,6,64]{1,3,2,0:T(8,128)(2,1)}, bf16[2,512,6,64]{1,3,2,0:T(8,128)(2,1)}, f32[2,512,6,64]{1,3,2,0:T(8,128)}, f32[2,6,512,51...) while((s32[]{:T(128)}, ...), condition=%wide.region_27.28_spmd, body=%wide.region_25.27_spmd.sunk | while | flops 1227224064 | bytes 94064864 | solution.py:276
  544.8 3.4 multiply_reduce_fusion.28
  548.1 4.2 bitcast_dynamic-update-slice_fusion.8
  562.7 3.4 multiply_reduce_fusion.28
  566.1 4.3 bitcast_dynamic-update-slice_fusion.8
  577.6 2.7 fusion.206
  586.7 2.7 stack_reshape.24
  592.2 5.6 bitcast_convert_fusion.1
  598.0 7.9 convolution_bitcast_fusion
  608.8 4.3 convolution_bitcast_fusion.4
  613.1 6.5 all-reduce.23.cloned.1.call-done
  619.7 5.1 multiply_reduce_fusion.4
  627.1 9.6 fusion.212
  638.3 3.7 fusion.152
  642.1 5.6 convolution_bitcast_fusion.1
  647.8 7.4 pad_maximum_fusion.1
  655.3 4.9 convolution_bitcast_fusion.3
  660.3 3.5 all-reduce.25.cloned.1.call-done
  663.8 4.8 multiply_reduce_fusion.5
  676.7 54.2 %while.57 = (s32[]{:T(128)}, bf16[2,512,6,64]{1,3,2,0:T(8,128)(2,1)}, bf16[2,512,6,64]{1,3,2,0:T(8,128)(2,1)}, f32[2,512,6,64]{1,3,2,0:T(8,128)}, bf16[2,512,6,6...) while((s32[]{:T(128)}, ...), condition=%wide.region_36.37_spmd, body=%wide.region_34.36_spmd.sunk | while | flops 1222512128 | bytes 87736576 | solution.py:276
  676.7 5.2 exponential_select_fusion.3
  681.9 7.6 fusion.310
  689.5 7.8 fusion.311
  703.8 5.2 exponential_select_fusion.3
  709.0 7.6 fusion.310
  716.6 7.8 fusion.311
  739.8 5.2 bitcast_convert_fusion
  745.3 8.5 pad_maximum_fusion
  760.5 3.3 pad_maximum_fusion.2
  767.6 3.6 add_reduce_fusion
  772.1 736.8 %all-reduce.31.cloned.1.call-done = (f32[2,768,3,384]{3,1,2,0:T(8,128)}, f32[2,768,384]{2,1,0:T(8,128)}, f32[2,768,1536]{2,1,0:T(8,128)}, f32[2,768,1536]{2,1,0:T(8,128)}) async-done(((f32[2,768,3,384]{3,1,2,0:T(8,128)}, f32[2,768,384]{2,1,0:T(8,128)}, f32[2,768,1536]{2,1,0:T(8,128)}, f32[2,768,1536]{2,1,0:T(8,128)}), (f32[2,768,3,384]{3,1,2,0:T(8,128)}, f32[2,768,384]{2,1,0:T(8,128)}, ...) | async-done | bytes 28311568 | tf_op jit(solution)/shard_map/psum | solution.py:323
  1518.5 114.0 %all-reduce.29.cloned.1.call-done = f32[2,8448]{1,0:T(2,128)} async-done(((f32[2,8448]{1,0:T(2,128)}), f32[2,8448]{1,0:T(2,128)}) %all-reduce.29.cloned.1.call-update) | async-done | bytes 67600 | tf_op jit(solution)/shard_map/psum | solution.py:337
  1634.1 42.6 %psum.124 = f32[]{:T(128)} all-reduce(f32[]{:T(128)S(6)} %add.424), channel_id=1, replica_groups=mesh['dp'=16,'tensor'=2] {'dp','tensor'}, use_global_device_ids=true, to_apply=%region_46.47 | all-reduce | flops 1 | bytes 8 | tf_op jit(solution)/shard_map/psum | solution.py:337
  1682.0 3.2 multiply_reduce_fusion.16
  1687.8 39.3 %all-reduce = (f32[4,2]{1,0:T(4,128)S(1)}, f32[4,2]{1,0:T(4,128)S(1)}) all-reduce(f32[4,2]{1,0:T(4,128)S(1)} %pad_maximum_fusion.12, f32[4,2]{1,0:T(4,128)S(1)} %pad_maximum_fusion.11), channel_id=1, replica_groups=mesh['dp'=16,'tensor'=2] {'dp','tensor'}, use_global_device_ids=true, to_apply=%region_74.75 | all-reduce | flops 16 | bytes 128 | tf_op jit(solution)/shard_map/psum | solution.py:353
  (526 shorter events, 188.6 us)
Async XLA Ops:
  7.2 78.1 %all-gather.5.cloned.1.call-start = ((), (), s32[]{:S(2)}) async-start(), calls=%async_computation | async-start | bytes 3760128 | tf_op jit(solution)/shard_map/all_gather | solution.py:137
  9.0 134.3 %all-gather.7.cloned.1.call-start = ((), (), s32[]{:S(2)}) async-start(), calls=%async_computation.1 | async-start | bytes 1253376 | tf_op jit(solution)/shard_map/all_gather | solution.py:138
  10.6 155.7 %all-reduce.13.cloned.1.call-start = ((), (), s32[]{:S(2)}) async-start(), calls=%async_computation.2 | async-start | bytes 3145728 | tf_op jit(solution)/shard_map/psum | solution.py:181
  12.2 347.3 %copy-start.73 = (f32[768]{0:T(1024)}, f32[768]{0:T(1024)S(1)}, u32[]{:S(2)}) copy-start(f32[768]{0:T(1024)S(1)} %get-tuple-element.433) | copy-start | bytes 9220
  12.2 347.3 %copy-start.82 = (f32[768]{0:T(1024)}, f32[768]{0:T(1024)S(1)}, u32[]{:S(2)}) copy-start(f32[768]{0:T(1024)S(1)} %get-tuple-element.432) | copy-start | bytes 9220
  12.2 347.3 %copy-start.100 = (f32[768]{0:T(1024)}, f32[768]{0:T(1024)S(1)}, u32[]{:S(2)}) copy-start(f32[768]{0:T(1024)S(1)} %get-tuple-element.431) | copy-start | bytes 9220
  12.2 409.8 %copy-start.86 = (f32[768]{0:T(1024)}, f32[768]{0:T(1024)S(1)}, u32[]{:S(2)}) copy-start(f32[768]{0:T(1024)S(1)} %get-tuple-element.429) | copy-start | bytes 9220
  12.2 409.8 %copy-start.102 = (f32[768]{0:T(1024)}, f32[768]{0:T(1024)S(1)}, u32[]{:S(2)}) copy-start(f32[768]{0:T(1024)S(1)} %get-tuple-element.428) | copy-start | bytes 9220
  114.9 28.3 %copy-start.20 = (bf16[2,512,6,64]{1,3,2,0:T(8,128)(2,1)}, bf16[2,512,6,64]{1,3,2,0:T(8,128)(2,1)S(1)}, u32[]{:S(2)}) copy-start(bf16[2,512,6,64]{1,3,2,0:T(8,128)(2,1)S(1)} %get-tuple-element.1014) | copy-start | bytes 2359300
  114.9 31.9 %copy-start.69 = (f32[2,6,512]{2,1,0:T(8,128)}, f32[2,6,512]{2,1,0:T(8,128)S(1)}, u32[]{:S(2)}) copy-start(f32[2,6,512]{2,1,0:T(8,128)S(1)} %get-tuple-element.954) | copy-start | bytes 73732
  116.8 32.0 %copy-start.32 = (f32[2,48,1536]{2,1,0:T(8,128)S(1)}, f32[2,48,1536]{2,1,0:T(8,128)}, u32[]{:S(2)}) copy-start(f32[2,48,1536]{2,1,0:T(8,128)} %param.32) | copy-start | bytes 1769476
  143.3 23.1 %copy-start.10 = (bf16[1024,768]{1,0:T(8,128)(2,1)S(1)}, bf16[1024,768]{1,0:T(8,128)(2,1)}, u32[]{:S(2)}) copy-start(bf16[1024,768]{1,0:T(8,128)(2,1)} %param.26) | copy-start | bytes 4718596
  146.9 104.6 %all-gather.9.cloned.1.call-start = ((), (), s32[]{:S(2)}) async-start(), calls=%async_computation.3 | async-start | bytes 5013504 | tf_op jit(solution)/shard_map/all_gather | solution.py:139
  148.8 185.2 %all-gather.11.cloned.1.call-start = ((), (), s32[]{:S(2)}) async-start(), calls=%async_computation.4 | async-start | bytes 5013504 | tf_op jit(solution)/shard_map/all_gather | solution.py:140
  149.6 209.9 %all-reduce.15.cloned.1.call-start = ((), (), s32[]{:S(2)}) async-start(), calls=%async_computation.5 | async-start | bytes 3145728 | tf_op jit(solution)/shard_map/psum | solution.py:194
  150.5 100.9 %copy-start.116 = (f32[1536]{0:T(1024)}, f32[1536]{0:T(1024)S(1)}, u32[]{:S(2)}) copy-start(f32[1536]{0:T(1024)S(1)} %dynamic-slice_reduce_fusion.5) | copy-start | bytes 18436
  168.5 191.1 %copy-start.76 = (f32[1024]{0:T(1024)}, f32[1024]{0:T(1024)S(1)}, u32[]{:S(2)}) copy-start(f32[1024]{0:T(1024)S(1)} %broadcast_multiply_fusion.3) | copy-start | bytes 12292
  169.4 102.9 %copy-start.92 = (f32[1024]{0:T(1024)}, f32[1024]{0:T(1024)S(1)}, u32[]{:S(2)}) copy-start(f32[1024]{0:T(1024)S(1)} %multiply_reduce_fusion.13) | copy-start | bytes 12292
  169.4 190.2 %copy-start.84 = (f32[1024]{0:T(1024)}, f32[1024]{0:T(1024)S(1)}, u32[]{:S(2)}) copy-start(f32[1024]{0:T(1024)S(1)} %fusion.167) | copy-start | bytes 12292
  340.4 81.7 %all-reduce.17.cloned.1.call-start = ((), (), s32[]{:S(2)}) async-start(), calls=%async_computation.6 | async-start | bytes 3145728 | tf_op jit(solution)/shard_map/psum | solution.py:181
  363.2 58.9 %copy-start.78 = (f32[1024]{0:T(1024)}, f32[1024]{0:T(1024)S(1)}, u32[]{:S(2)}) copy-start(f32[1024]{0:T(1024)S(1)} %broadcast_multiply_fusion.2) | copy-start | bytes 12292
  363.7 58.4 %copy-start.89 = (f32[1024]{0:T(1024)}, f32[1024]{0:T(1024)S(1)}, u32[]{:S(2)}) copy-start(f32[1024]{0:T(1024)S(1)} %fusion.168) | copy-start | bytes 12292
  397.1 25.0 %copy-start.106 = (f32[768]{0:T(1024)S(1)}, f32[768]{0:T(1024)}, u32[]{:S(2)}) copy-start(f32[768]{0:T(1024)} %get-tuple-element.427) | copy-start | bytes 9220
  400.3 73.6 %all-reduce.19.cloned.1.call-start = ((), (), s32[]{:S(2)}) async-start(), calls=%async_computation.7 | async-start | bytes 3145728 | tf_op jit(solution)/shard_map/psum | solution.py:194
  425.8 19.4 %copy-start.3 = (f32[1024,768]{1,0:T(8,128)}, f32[1024,768]{1,0:T(8,128)S(1)}, u32[]{:S(2)}) copy-start(f32[1024,768]{1,0:T(8,128)S(1)} %get-tuple-element.545) | copy-start | bytes 9437188
  446.8 27.2 %copy-start.105 = (f32[768]{0:T(1024)S(1)}, f32[768]{0:T(1024)}, u32[]{:S(2)}) copy-start(f32[768]{0:T(1024)} %get-tuple-element.424) | copy-start | bytes 9220
  452.2 68.9 %all-reduce.21.cloned.1.call-start = ((), (), s32[]{:S(2)}) async-start(), calls=%async_computation.8 | async-start | bytes 3145728 | tf_op jit(solution)/shard_map/psum | solution.py:246
  473.9 10.4 slice-start.8
  481.4 14.2 slice-start.4
  484.4 9.6 copy-start.8
  484.4 11.2 slice-start.5
  499.3 120.3 %all-reduce.23.cloned.1.call-start = ((), (), s32[]{:S(2)}) async-start(), calls=%async_computation.9 | async-start | bytes 3145728 | tf_op jit(solution)/shard_map/psum | solution.py:293
  582.6 7.9 copy-start.40
  597.9 7.9 copy-start.53
  597.9 65.9 %all-reduce.25.cloned.1.call-start = ((), (), s32[]{:S(2)}) async-start(), calls=%async_computation.10 | async-start | bytes 3145728 | tf_op jit(solution)/shard_map/psum | solution.py:246
  598.0 7.9 copy-start.18
  598.0 10.3 copy-start.63
  613.1 11.7 copy-start.95
  625.2 13.1 slice-start.6
  627.1 9.6 copy-start.6
  627.1 11.3 slice-start.7
  642.1 125.4 %all-reduce.27.cloned.1.call-start = ((), (), s32[]{:S(2)}) async-start(), calls=%async_computation.11 | async-start | bytes 3145728 | tf_op jit(solution)/shard_map/psum | solution.py:293
  647.8 7.5 copy-start.11
  647.8 7.5 copy-start.14
  647.8 7.5 copy-start.74
  647.8 7.5 copy-start.77
  647.8 7.5 copy-start.83
  660.3 8.4 copy-start.93
  681.9 19.8 %slice-start = ((s8[6291456]{0:T(1024)(128)(4,1)}), s8[2097152]{0:T(1024)(128)(4,1)S(1)}, s32[]{:S(2)}) async-start(s8[6291456]{0:T(1024)(128)(4,1)} %bitcast.400), calls=%async_computation.14 | async-start | bytes 4194304 | tf_op jit(solution)/shard_map/while
  689.5 12.2 slice-start.1
  709.0 19.8 %slice-start = ((s8[6291456]{0:T(1024)(128)(4,1)}), s8[2097152]{0:T(1024)(128)(4,1)S(1)}, s32[]{:S(2)}) async-start(s8[6291456]{0:T(1024)(128)(4,1)} %bitcast.400), calls=%async_computation.14 | async-start | bytes 4194304 | tf_op jit(solution)/shard_map/while
  716.6 12.2 slice-start.1
  736.6 8.4 copy-start.57
  745.0 8.8 copy-start.26
  745.0 763.9 %all-reduce.31.cloned.1.call-start = ((), (), s32[]{:S(2)}) async-start(), calls=%async_computation.13 | async-start | bytes 56623104 | tf_op jit(solution)/shard_map/psum | solution.py:323
  745.3 8.5 copy-start.51
  763.9 868.6 %all-reduce.29.cloned.1.call-start = ((), (), s32[]{:S(2)}) async-start(), calls=%async_computation.12 | async-start | bytes 135168 | tf_op jit(solution)/shard_map/psum | solution.py:337
  767.5 910.6 %copy-start.47 = (f32[2,48,384]{2,1,0:T(8,128)S(1)}, f32[2,48,384]{2,1,0:T(8,128)}, u32[]{:S(2)}) copy-start(f32[2,48,384]{2,1,0:T(8,128)} %param.30) | copy-start | bytes 442372
  771.2 908.8 %copy-start.34 = (f32[2,48,1536]{2,1,0:T(8,128)S(1)}, f32[2,48,1536]{2,1,0:T(8,128)}, u32[]{:S(2)}) copy-start(f32[2,48,1536]{2,1,0:T(8,128)} %param.31) | copy-start | bytes 1769476
  771.2 908.8 %copy-start.66 = (f32[2,48,1536]{2,1,0:T(8,128)S(1)}, f32[2,48,1536]{2,1,0:T(8,128)}, u32[]{:S(2)}) copy-start(f32[2,48,1536]{2,1,0:T(8,128)} %param.38) | copy-start | bytes 1769476
  1508.9 173.1 %copy-start.33 = (f32[2,48,1536]{2,1,0:T(8,128)S(1)}, f32[2,48,1536]{2,1,0:T(8,128)}, u32[]{:S(2)}) copy-start(f32[2,48,1536]{2,1,0:T(8,128)} %param.32) | copy-start | bytes 1769476
  1682.0 47.4 %copy-start.42 = (f32[2,48,1536]{2,1,0:T(8,128)}, f32[2,48,1536]{2,1,0:T(8,128)S(1)}, u32[]{:S(2)}) copy-start(f32[2,48,1536]{2,1,0:T(8,128)S(1)} %get-tuple-element.528) | copy-start | bytes 1769476
  1682.0 47.4 %copy-start.43 = (f32[2,48,1536]{2,1,0:T(8,128)}, f32[2,48,1536]{2,1,0:T(8,128)S(1)}, u32[]{:S(2)}) copy-start(f32[2,48,1536]{2,1,0:T(8,128)S(1)} %get-tuple-element.529) | copy-start | bytes 1769476
  1685.2 45.4 %copy-start.44 = (f32[2,48,1536]{2,1,0:T(8,128)}, f32[2,48,1536]{2,1,0:T(8,128)S(1)}, u32[]{:S(2)}) copy-start(f32[2,48,1536]{2,1,0:T(8,128)S(1)} %get-tuple-element.530) | copy-start | bytes 1769476
  (95 other events, 299.0 us)
Sparse Core Ops, SparseCore 0:
  11.3 73.9 all-gather.4
  88.5 54.6 all-gather.6
  147.0 19.2 all-reduce.12
  169.8 81.6 all-gather.8
  255.0 78.9 all-gather.10
  340.5 19.0 all-reduce.14
  400.5 21.5 all-reduce.16
  452.3 21.5 all-reduce.18
  499.5 21.5 all-reduce.20
  598.0 21.5 all-reduce.22
  642.2 21.5 all-reduce.24
  745.1 21.5 all-reduce.26
  773.2 735.7 all-reduce.30
  1515.9 116.6 all-reduce.28
where the time goes:
time: 1750 us; the launch traced here: 1740 us
  waiting for transfers between devices  1190 us (68%)
  matrix products  238 us (14%)
  other arithmetic  120 us (7%)
  local copies, waits for them, and re-layouts  86.9 us (5%)
  blocking collectives  81.9 us (5%)
  between operations  20.9 us (1%)
    psum x1, waiting for transfers between devices, local(): lax.psum((big_totals[0], big_totals[1], big_totals[2], big_totals[3]), 'dp')  737 us
    psum x1, waiting for transfers between devices, local(): lax.psum((square_part, weight_square, small_partial), ('dp', 'tensor'))  114 us
    all_gather x1, waiting for transfers between devices, local(): lax.all_gather(up_weight.astype(jnp.bfloat16), 'dp', axis=1, tiled=True)  82.1 us
    all_gather x1, waiting for transfers between devices, local(): lax.all_gather(proj_weight.astype(jnp.bfloat16), 'dp', axis=1, tiled=True)  72.2 us
    all_gather x1, waiting for transfers between devices, local(): lax.all_gather(down_weight.astype(jnp.bfloat16), 'dp', axis=1, tiled=True)  61.6 us
    psum x1, blocking collectives, local(): lax.psum((square_part, weight_square, small_partial), ('dp', 'tensor'))  42.6 us
    psum x2, waiting for transfers between devices, local(): lax.psum(jnp.einsum('tf,df->td', act_low, down_full[layer_at], preferred_...  40.7 us
    dot_general x2, matrix products, local(): jnp.einsum('td,df->tf', first_low, up_full[layer_at], preferred_element_t...  39.4 us
  transfers between devices with their start and end apart: 14, of which 13 were waited for; matrix products, arithmetic and copies ran while one was open for 8% of the time, Pallas kernels for 0%

commit v1 on v0

--- a/solution.py
+++ b/solution.py
@@ -350,7 +350,8 @@
     update_square = jnp.stack(
         [jnp.sum(update * update, axis=tuple(range(1, update.ndim))) for update in updates]
     )
-    update_square = lax.psum(update_square, ("dp", "tensor"))
+    r_now = jax.lax.all_gather(update_square, ("dp", "tensor"))
+    update_square = jnp.sum(r_now, axis=0)
     ratio = jnp.sqrt(weight_square) / jnp.sqrt(update_square)
     outputs = [hidden, grad_rows, grad_norm]
     for kind_at in range(4):

time: 1750 us -> 1780 us (1.017)
  blocking collectives: 81.9 us -> 123 us
    all_gather x0 -> x1, blocking collectives: none -> 41.2 us  [local(): r_now = jax.lax.all_gather(update_square, ('dp', 'tensor'))]
    psum x1 -> x0, blocking collectives: 39.3 us -> none  [local(): update_square = lax.psum(update_square, ('dp', 'tensor'))]
    psum x1 -> x2, blocking collectives: 42.6 us -> 81.8 us  [local(): lax.psum((square_part, weight_square, small_partial), ('dp', 'tensor'))]
  transfers between devices with their start and end apart: 14 -> 14, of which waited for: 13 -> 14; matrix products, arithmetic and copies ran while one was open for 8% -> 7% of each run, Pallas kernels for 0% -> 0%
where the time goes in v1:
time: 1780 us; the launch traced here: 1770 us
  waiting for transfers between devices  1200 us (67%)
  matrix products  237 us (13%)
  blocking collectives  123 us (7%)
  other arithmetic  120 us (7%)
  local copies, waits for them, and re-layouts  72.9 us (4%)
  between operations  20.9 us (1%)
    psum x1, waiting for transfers between devices, local(): lax.psum((big_totals[0], big_totals[1], big_totals[2], big_totals[3]), 'dp')  737 us
    psum x1, waiting for transfers between devices, local(): lax.psum((square_part, weight_square, small_partial), ('dp', 'tensor'))  114 us
    all_gather x1, waiting for transfers between devices, local(): lax.all_gather(up_weight.astype(jnp.bfloat16), 'dp', axis=1, tiled=True)  82.1 us
    psum x2, blocking collectives, local(): lax.psum((square_part, weight_square, small_partial), ('dp', 'tensor'))  81.8 us
    all_gather x1, waiting for transfers between devices, local(): lax.all_gather(proj_weight.astype(jnp.bfloat16), 'dp', axis=1, tiled=True)  71.6 us
    all_gather x1, waiting for transfers between devices, local(): lax.all_gather(down_weight.astype(jnp.bfloat16), 'dp', axis=1, tiled=True)  62 us
    all_gather x1, blocking collectives, local(): r_now = jax.lax.all_gather(update_square, ('dp', 'tensor'))  41.2 us
    psum x2, waiting for transfers between devices, local(): lax.psum(jnp.einsum('tf,df->td', act_low, down_full[layer_at], preferred_...  40.5 us
  transfers between devices with their start and end apart: 14, of which 14 were waited for; matrix products, arithmetic and copies ran while one was open for 7% of the time, Pallas kernels for 0%

profile of v1, /device:TPU:0, one launch (start us, length us, event | category | flops | bytes accessed | tf_op | source)
XLA Modules:
  0.0 1774.6 jit_solution(389258067271844284)
XLA Ops:
  13.7 71.6 %all-gather.7.cloned.1.call-done = bf16[2,768,3,384]{3,1,2,0:T(8,128)(2,1)} async-done(((bf16[2,48,3,384]{3,1,2,0:T(8,128)(2,1)}), bf16[2,768,3,384]{3,1,2,0:T(8,128)(2,1)}) %all-gather.7.cloned.1.call-update) | async-done | bytes 3538960 | tf_op jit(solution)/shard_map/all_gather | solution.py:137
  85.3 5.6 fusion.209
  92.6 2.8 squeeze.116
  100.1 11.4 while.54
  113.4 29.9 %all-gather.9.cloned.1.call-done = bf16[2,768,384]{2,1,0:T(8,128)(2,1)} async-done(((bf16[2,48,384]{2,1,0:T(8,128)(2,1)}), bf16[2,768,384]{2,1,0:T(8,128)(2,1)}) %all-gather.9.cloned.1.call-update) | async-done | bytes 1179664 | tf_op jit(solution)/shard_map/all_gather | solution.py:138
  143.3 3.6 convolution_convert_fusion.1
  149.7 16.6 all-reduce.12.cloned.1.call-done
  169.4 82.1 %all-gather.11.cloned.1.call-done = bf16[2,768,1536]{2,1,0:T(8,128)(2,1)} async-done(((bf16[2,48,1536]{2,1,0:T(8,128)(2,1)}), bf16[2,768,1536]{2,1,0:T(8,128)(2,1)}) %all-gather.11.cloned.1.call-update) | async-done | bytes 4718608 | tf_op jit(solution)/shard_map/all_gather | solution.py:139
  251.5 20.6 %multiply_convert_fusion.1 = (bf16[1024,1536]{1,0:T(8,128)(2,1)}, f32[1024,1536]{1,0:T(8,128)}, f32[1024,1536]{1,0:T(8,128)}) fusion(f32[1536]{0:T(1024)S(1)} %dynamic-slice_reduce_fusion.5, bf16[2,768,1536]{2,1,0:T(8,128)(2,1)} %all-gather.11.cloned.1.call-done, f32[768]{0:T(1024)S(1)} %copy-done.88, f32[768]{0:T(1024)S(1)} %get-tuple-element.548, ...), kind=kOutput, calls=%fused_computation.155 | convolution fusion | flops 2526806016 | bytes 21257216 | tf_op jit(solution)/shard_map/td,df->tf/dot_general | solution.py:190
  272.1 62.0 %all-gather.13.cloned.1.call-done = bf16[2,768,1536]{2,1,0:T(8,128)(2,1)} async-done(((bf16[2,48,1536]{2,1,0:T(8,128)(2,1)}), bf16[2,768,1536]{2,1,0:T(8,128)(2,1)}) %all-gather.13.cloned.1.call-update) | async-done | bytes 4718608 | tf_op jit(solution)/shard_map/all_gather | solution.py:140
  334.1 6.4 fusion.151
  340.9 18.8 %all-reduce.14.cloned.1.call-done = bf16[1024,768]{1,0:T(8,128)(2,1)} async-done(((bf16[1024,768]{1,0:T(8,128)(2,1)}), bf16[1024,768]{1,0:T(8,128)(2,1)}) %all-reduce.14.cloned.1.call-update) | async-done | bytes 1572880 | tf_op jit(solution)/shard_map/psum | solution.py:194
  359.7 3.3 fusion.200
  363.8 3.8 fusion.210
  380.8 13.8 while.55
  382.3 2.8 fusion.280
  389.0 2.8 fusion.280
  400.2 21.6 %all-reduce.16.cloned.1.call-done = bf16[1024,768]{1,0:T(8,128)(2,1)} async-done(((bf16[1024,768]{1,0:T(8,128)(2,1)}), bf16[1024,768]{1,0:T(8,128)(2,1)}) %all-reduce.16.cloned.1.call-update) | async-done | bytes 1572880 | tf_op jit(solution)/shard_map/psum | solution.py:181
  421.9 3.6 fusion.199
  426.3 18.7 %multiply_convert_fusion = (bf16[1024,1536]{1,0:T(8,128)(2,1)S(1)}, f32[1024,1536]{1,0:T(8,128)}, f32[1024,1536]{1,0:T(8,128)}) fusion(f32[1536]{0:T(1024)S(1)} %dynamic-slice_reduce_fusion.4, bf16[2,768,1536]{2,1,0:T(8,128)(2,1)S(1)} %bitcast.411, f32[1024,768]{1,0:T(8,128)S(1)} %get-tuple-element.663, f32[768]{0:T(1024)S(1)} %copy-done.92, ...), kind=kOutput, calls=%fused_computation.142 | convolution fusion | flops 2523660288 | bytes 21258240 | tf_op jit(solution)/shard_map/td,df->tf/dot_general | solution.py:190
  446.7 5.4 fusion.149
  452.1 21.7 %all-reduce.18.cloned.1.call-done = bf16[1024,768]{1,0:T(8,128)(2,1)} async-done(((bf16[1024,768]{1,0:T(8,128)(2,1)}), bf16[1024,768]{1,0:T(8,128)(2,1)}) %all-reduce.18.cloned.1.call-update) | async-done | bytes 1572880 | tf_op jit(solution)/shard_map/psum | solution.py:194
  473.8 3.6 fusion.197
  481.3 2.9 fusion.196
  484.3 9.5 fusion.211
  495.5 3.7 fusion.150
  502.1 8.0 convolution_bitcast_fusion.2
  510.1 10.9 all-reduce.20.cloned.1.call-done
  521.0 4.9 multiply_reduce_fusion.3
  537.5 36.2 %while.56 = (s32[]{:T(128)}, bf16[2,512,6,64]{1,3,2,0:T(8,128)(2,1)}, bf16[2,512,6,64]{1,3,2,0:T(8,128)(2,1)}, f32[2,512,6,64]{1,3,2,0:T(8,128)}, f32[2,6,512,51...) while((s32[]{:T(128)}, ...), condition=%wide.region_27.28_spmd, body=%wide.region_25.27_spmd.sunk | while | flops 1227224064 | bytes 90919112 | solution.py:276
  541.0 3.4 multiply_reduce_fusion.28
  544.3 4.2 bitcast_dynamic-update-slice_fusion.8
  558.8 3.4 multiply_reduce_fusion.28
  562.1 4.2 bitcast_dynamic-update-slice_fusion.8
  573.7 2.7 fusion.206
  583.3 5.4 bitcast_convert_fusion.1
  589.0 7.9 convolution_bitcast_fusion
  599.9 4.4 convolution_bitcast_fusion.4
  604.3 6.2 all-reduce.22.cloned.1.call-done
  610.5 4.9 multiply_reduce_fusion.4
  617.9 9.6 fusion.212
  629.2 3.7 fusion.152
  633.0 5.6 convolution_bitcast_fusion.1
  638.7 7.4 pad_maximum_fusion.1
  646.2 4.9 convolution_bitcast_fusion.3
  651.1 3.5 all-reduce.24.cloned.1.call-done
  654.7 4.2 multiply_reduce_fusion.5
  667.3 54.3 %while.57 = (s32[]{:T(128)}, bf16[2,512,6,64]{1,3,2,0:T(8,128)(2,1)}, bf16[2,512,6,64]{1,3,2,0:T(8,128)(2,1)}, f32[2,512,6,64]{1,3,2,0:T(8,128)}, bf16[2,512,6,6...) while((s32[]{:T(128)}, ...), condition=%wide.region_36.37_spmd, body=%wide.region_34.36_spmd.sunk | while | flops 1222512128 | bytes 87736576 | solution.py:276
  667.4 5.2 exponential_select_fusion.3
  672.6 7.6 fusion.310
  680.2 7.8 fusion.311
  694.4 5.2 exponential_select_fusion.3
  699.7 7.6 fusion.310
  707.3 7.8 fusion.311
  730.3 5.2 bitcast_convert_fusion
  735.8 8.5 pad_maximum_fusion
  750.5 3.3 pad_maximum_fusion.2
  757.3 4.5 add_reduce_fusion
  762.6 736.8 %all-reduce.30.cloned.1.call-done = (f32[2,768,3,384]{3,1,2,0:T(8,128)}, f32[2,768,384]{2,1,0:T(8,128)}, f32[2,768,1536]{2,1,0:T(8,128)}, f32[2,768,1536]{2,1,0:T(8,128)}) async-done(((f32[2,768,3,384]{3,1,2,0:T(8,128)}, f32[2,768,384]{2,1,0:T(8,128)}, f32[2,768,1536]{2,1,0:T(8,128)}, f32[2,768,1536]{2,1,0:T(8,128)}), (f32[2,768,3,384]{3,1,2,0:T(8,128)}, f32[2,768,384]{2,1,0:T(8,128)}, ...) | async-done | bytes 28311568 | tf_op jit(solution)/shard_map/psum | solution.py:323
  1509.1 114.0 %all-reduce.28.cloned.1.call-done = f32[2,8448]{1,0:T(2,128)} async-done(((f32[2,8448]{1,0:T(2,128)}), f32[2,8448]{1,0:T(2,128)}) %all-reduce.28.cloned.1.call-update) | async-done | bytes 67600 | tf_op jit(solution)/shard_map/psum | solution.py:337
  1624.7 42.6 %psum.117 = f32[]{:T(128)} all-reduce(f32[]{:T(128)S(6)} %add.422), channel_id=1, replica_groups=mesh['dp'=16,'tensor'=2] {'dp','tensor'}, use_global_device_ids=true, to_apply=%region_46.47 | all-reduce | flops 1 | bytes 8 | tf_op jit(solution)/shard_map/psum | solution.py:337
  1672.7 3.3 multiply_reduce_fusion.16
  1678.7 39.2 %psum.119 = f32[4,2]{0,1:T(2,128)S(1)} all-reduce(f32[4,2]{0,1:T(2,128)S(1)} %pad_maximum_fusion.12), channel_id=1, replica_groups=mesh['dp'=16,'tensor'=2] {'dp','tensor'}, use_global_device_ids=true, to_apply=%region_69.70 | all-reduce | flops 8 | bytes 64 | tf_op jit(solution)/shard_map/psum | solution.py:337
  1718.0 41.2 %all-gather.1 = f32[32,4,2]{1,2,0:T(2,128)S(1)} all-gather(f32[1,4,2]{1,2,0:T(2,128)S(1)} %bitcast.401), channel_id=2, replica_groups=mesh['dp'=16,'tensor'=2] {'dp','tensor'}, dimensions={0}, use_global_device_ids=true | all-gather | bytes 1056 | tf_op jit(solution)/shard_map/all_gather | solution.py:353
  (509 shorter events, 179.5 us)
Async XLA Ops:
  7.2 78.1 %all-gather.7.cloned.1.call-start = ((), (), s32[]{:S(2)}) async-start(), calls=%async_computation | async-start | bytes 3760128 | tf_op jit(solution)/shard_map/all_gather | solution.py:137
  9.0 134.3 %all-gather.9.cloned.1.call-start = ((), (), s32[]{:S(2)}) async-start(), calls=%async_computation.1 | async-start | bytes 1253376 | tf_op jit(solution)/shard_map/all_gather | solution.py:138
  10.6 155.7 %all-reduce.12.cloned.1.call-start = ((), (), s32[]{:S(2)}) async-start(), calls=%async_computation.2 | async-start | bytes 3145728 | tf_op jit(solution)/shard_map/psum | solution.py:181
  12.3 347.5 %copy-start.63 = (f32[768]{0:T(1024)}, f32[768]{0:T(1024)S(1)}, u32[]{:S(2)}) copy-start(f32[768]{0:T(1024)S(1)} %get-tuple-element.549) | copy-start | bytes 9220
  12.3 347.5 %copy-start.73 = (f32[768]{0:T(1024)}, f32[768]{0:T(1024)S(1)}, u32[]{:S(2)}) copy-start(f32[768]{0:T(1024)S(1)} %get-tuple-element.548) | copy-start | bytes 9220
  12.3 409.6 %copy-start.77 = (f32[768]{0:T(1024)}, f32[768]{0:T(1024)S(1)}, u32[]{:S(2)}) copy-start(f32[768]{0:T(1024)S(1)} %get-tuple-element.545) | copy-start | bytes 9220
  111.5 31.8 %copy-start.19 = (bf16[2,512,6,64]{1,3,2,0:T(8,128)(2,1)}, bf16[2,512,6,64]{1,3,2,0:T(8,128)(2,1)S(1)}, u32[]{:S(2)}) copy-start(bf16[2,512,6,64]{1,3,2,0:T(8,128)(2,1)S(1)} %get-tuple-element.1128) | copy-start | bytes 2359300
  112.4 34.6 %copy-start.33 = (f32[2,48,1536]{2,1,0:T(8,128)S(1)}, f32[2,48,1536]{2,1,0:T(8,128)}, u32[]{:S(2)}) copy-start(f32[2,48,1536]{2,1,0:T(8,128)} %param.31) | copy-start | bytes 1769476
  113.4 34.4 %copy-start.31 = (f32[2,48,1536]{2,1,0:T(8,128)S(1)}, f32[2,48,1536]{2,1,0:T(8,128)}, u32[]{:S(2)}) copy-start(f32[2,48,1536]{2,1,0:T(8,128)} %param.32) | copy-start | bytes 1769476
  143.3 23.1 %copy-start.10 = (bf16[1024,768]{1,0:T(8,128)(2,1)S(1)}, bf16[1024,768]{1,0:T(8,128)(2,1)}, u32[]{:S(2)}) copy-start(bf16[1024,768]{1,0:T(8,128)(2,1)} %param.26) | copy-start | bytes 4718596
  146.9 104.6 %all-gather.11.cloned.1.call-start = ((), (), s32[]{:S(2)}) async-start(), calls=%async_computation.3 | async-start | bytes 5013504 | tf_op jit(solution)/shard_map/all_gather | solution.py:139
  147.7 186.4 %all-gather.13.cloned.1.call-start = ((), (), s32[]{:S(2)}) async-start(), calls=%async_computation.4 | async-start | bytes 5013504 | tf_op jit(solution)/shard_map/all_gather | solution.py:140
  148.5 211.2 %all-reduce.14.cloned.1.call-start = ((), (), s32[]{:S(2)}) async-start(), calls=%async_computation.5 | async-start | bytes 3145728 | tf_op jit(solution)/shard_map/psum | solution.py:194
  149.7 101.8 %copy-start.105 = (f32[1536]{0:T(1024)}, f32[1536]{0:T(1024)S(1)}, u32[]{:S(2)}) copy-start(f32[1536]{0:T(1024)S(1)} %dynamic-slice_reduce_fusion.5) | copy-start | bytes 18436
  166.3 85.2 %copy-start.88 = (f32[768]{0:T(1024)S(1)}, f32[768]{0:T(1024)}, u32[]{:S(2)}) copy-start(f32[768]{0:T(1024)} %get-tuple-element.547) | copy-start | bytes 9220
  168.5 191.3 %copy-start.67 = (f32[1024]{0:T(1024)}, f32[1024]{0:T(1024)S(1)}, u32[]{:S(2)}) copy-start(f32[1024]{0:T(1024)S(1)} %broadcast_multiply_fusion.3) | copy-start | bytes 12292
  169.4 102.8 %copy-start.83 = (f32[1024]{0:T(1024)}, f32[1024]{0:T(1024)S(1)}, u32[]{:S(2)}) copy-start(f32[1024]{0:T(1024)S(1)} %multiply_reduce_fusion.13) | copy-start | bytes 12292
  169.4 190.3 %copy-start.75 = (f32[1024]{0:T(1024)}, f32[1024]{0:T(1024)S(1)}, u32[]{:S(2)}) copy-start(f32[1024]{0:T(1024)S(1)} %fusion.167) | copy-start | bytes 12292
  334.1 25.6 %copy-start.95 = (f32[768]{0:T(1024)S(1)}, f32[768]{0:T(1024)}, u32[]{:S(2)}) copy-start(f32[768]{0:T(1024)} %get-tuple-element.546) | copy-start | bytes 9220
  340.5 81.3 %all-reduce.16.cloned.1.call-start = ((), (), s32[]{:S(2)}) async-start(), calls=%async_computation.6 | async-start | bytes 3145728 | tf_op jit(solution)/shard_map/psum | solution.py:181
  363.1 58.8 %copy-start.69 = (f32[1024]{0:T(1024)}, f32[1024]{0:T(1024)S(1)}, u32[]{:S(2)}) copy-start(f32[1024]{0:T(1024)S(1)} %broadcast_multiply_fusion.2) | copy-start | bytes 12292
  363.6 58.3 %copy-start.80 = (f32[1024]{0:T(1024)}, f32[1024]{0:T(1024)S(1)}, u32[]{:S(2)}) copy-start(f32[1024]{0:T(1024)S(1)} %fusion.168) | copy-start | bytes 12292
  396.9 25.0 %copy-start.94 = (f32[768]{0:T(1024)S(1)}, f32[768]{0:T(1024)}, u32[]{:S(2)}) copy-start(f32[768]{0:T(1024)} %get-tuple-element.543) | copy-start | bytes 9220
  400.1 73.7 %all-reduce.18.cloned.1.call-start = ((), (), s32[]{:S(2)}) async-start(), calls=%async_computation.7 | async-start | bytes 3145728 | tf_op jit(solution)/shard_map/psum | solution.py:194
  425.5 19.5 %copy-start.3 = (f32[1024,768]{1,0:T(8,128)}, f32[1024,768]{1,0:T(8,128)S(1)}, u32[]{:S(2)}) copy-start(f32[1024,768]{1,0:T(8,128)S(1)} %get-tuple-element.663) | copy-start | bytes 9437188
  446.7 27.1 %copy-start.93 = (f32[768]{0:T(1024)S(1)}, f32[768]{0:T(1024)}, u32[]{:S(2)}) copy-start(f32[768]{0:T(1024)} %get-tuple-element.540) | copy-start | bytes 9220
  452.1 68.9 %all-reduce.20.cloned.1.call-start = ((), (), s32[]{:S(2)}) async-start(), calls=%async_computation.8 | async-start | bytes 3145728 | tf_op jit(solution)/shard_map/psum | solution.py:246
  473.8 10.4 slice-start.8
  481.3 14.2 slice-start.4
  484.2 9.6 copy-start.8
  484.3 11.2 slice-start.5
  499.2 111.2 %all-reduce.22.cloned.1.call-start = ((), (), s32[]{:S(2)}) async-start(), calls=%async_computation.9 | async-start | bytes 3145728 | tf_op jit(solution)/shard_map/psum | solution.py:293
  499.4 10.8 copy-start.20
  588.8 8.1 copy-start.52
  588.8 65.9 %all-reduce.24.cloned.1.call-start = ((), (), s32[]{:S(2)}) async-start(), calls=%async_computation.10 | async-start | bytes 3145728 | tf_op jit(solution)/shard_map/psum | solution.py:246
  589.0 7.9 copy-start.17
  604.2 11.2 copy-start.86
  616.1 13.1 slice-start.6
  617.9 9.6 copy-start.6
  617.9 11.3 slice-start.7
  632.9 124.3 %all-reduce.26.cloned.1.call-start = ((), (), s32[]{:S(2)}) async-start(), calls=%async_computation.11 | async-start | bytes 3145728 | tf_op jit(solution)/shard_map/psum | solution.py:293
  638.6 7.5 copy-start.11
  638.6 7.5 copy-start.14
  638.6 7.5 copy-start.64
  638.6 7.5 copy-start.68
  638.6 7.5 copy-start.74
  638.7 7.5 copy-start.76
  651.1 7.8 copy-start.84
  672.6 19.9 %slice-start = ((s8[6291456]{0:T(1024)(128)(4,1)}), s8[2097152]{0:T(1024)(128)(4,1)S(1)}, s32[]{:S(2)}) async-start(s8[6291456]{0:T(1024)(128)(4,1)} %bitcast.393), calls=%async_computation.14 | async-start | bytes 4194304 | tf_op jit(solution)/shard_map/while
  680.2 12.3 slice-start.1
  699.7 19.9 %slice-start = ((s8[6291456]{0:T(1024)(128)(4,1)}), s8[2097152]{0:T(1024)(128)(4,1)S(1)}, s32[]{:S(2)}) async-start(s8[6291456]{0:T(1024)(128)(4,1)} %bitcast.393), calls=%async_computation.14 | async-start | bytes 4194304 | tf_op jit(solution)/shard_map/while
  707.2 12.3 slice-start.1
  735.5 8.8 copy-start.50
  735.6 763.9 %all-reduce.30.cloned.1.call-start = ((), (), s32[]{:S(2)}) async-start(), calls=%async_computation.13 | async-start | bytes 56623104 | tf_op jit(solution)/shard_map/psum | solution.py:323
  735.8 8.5 copy-start.25
  753.9 869.2 %all-reduce.28.cloned.1.call-start = ((), (), s32[]{:S(2)}) async-start(), calls=%async_computation.12 | async-start | bytes 135168 | tf_op jit(solution)/shard_map/psum | solution.py:337
  755.8 912.9 %copy-start.46 = (f32[2,48,384]{2,1,0:T(8,128)S(1)}, f32[2,48,384]{2,1,0:T(8,128)}, u32[]{:S(2)}) copy-start(f32[2,48,384]{2,1,0:T(8,128)} %param.30) | copy-start | bytes 442372
  755.8 912.9 %copy-start.65 = (f32[2,48,384]{2,1,0:T(8,128)S(1)}, f32[2,48,384]{2,1,0:T(8,128)}, u32[]{:S(2)}) copy-start(f32[2,48,384]{2,1,0:T(8,128)} %param.36) | copy-start | bytes 442372
  755.8 912.9 %copy-start.66 = (f32[2,48,384]{2,1,0:T(8,128)S(1)}, f32[2,48,384]{2,1,0:T(8,128)}, u32[]{:S(2)}) copy-start(f32[2,48,384]{2,1,0:T(8,128)} %param.37) | copy-start | bytes 442372
  761.8 908.7 %copy-start.34 = (f32[2,48,1536]{2,1,0:T(8,128)S(1)}, f32[2,48,1536]{2,1,0:T(8,128)}, u32[]{:S(2)}) copy-start(f32[2,48,1536]{2,1,0:T(8,128)} %param.31) | copy-start | bytes 1769476
  1499.5 173.2 %copy-start.32 = (f32[2,48,1536]{2,1,0:T(8,128)S(1)}, f32[2,48,1536]{2,1,0:T(8,128)}, u32[]{:S(2)}) copy-start(f32[2,48,1536]{2,1,0:T(8,128)} %param.32) | copy-start | bytes 1769476
  1672.6 89.3 %copy-start.42 = (f32[2,48,1536]{2,1,0:T(8,128)}, f32[2,48,1536]{2,1,0:T(8,128)S(1)}, u32[]{:S(2)}) copy-start(f32[2,48,1536]{2,1,0:T(8,128)S(1)} %get-tuple-element.646) | copy-start | bytes 1769476
  1672.6 89.3 %copy-start.43 = (f32[2,48,1536]{2,1,0:T(8,128)}, f32[2,48,1536]{2,1,0:T(8,128)S(1)}, u32[]{:S(2)}) copy-start(f32[2,48,1536]{2,1,0:T(8,128)S(1)} %get-tuple-element.647) | copy-start | bytes 1769476
  1678.5 87.3 %copy-start.44 = (f32[2,48,3,384]{3,1,2,0:T(8,128)}, f32[2,48,3,384]{3,1,2,0:T(8,128)S(1)}, u32[]{:S(2)}) copy-start(f32[2,48,3,384]{3,1,2,0:T(8,128)S(1)} %get-tuple-element.642) | copy-start | bytes 1327108
  (83 other events, 265.6 us)
Sparse Core Ops, SparseCore 0:
  11.3 73.9 all-gather.6
  88.5 54.6 all-gather.8
  147.0 19.2 all-reduce.11
  169.8 81.6 all-gather.10
  255.0 79.0 all-gather.12
  340.7 19.0 all-reduce.13
  400.2 21.5 all-reduce.15
  452.2 21.5 all-reduce.17
  499.4 21.5 all-reduce.19
  588.9 21.5 all-reduce.21
  633.1 21.5 all-reduce.23
  735.7 21.5 all-reduce.25
  763.7 735.7 all-reduce.29
  1506.4 116.6 all-reduce.27
